TPU v7x, 32 devices: a whole 2x2x4 slice. The times are simulated.
32 devices in a mesh: seq: 8 (over z, core), fsdp: 4 (over y, x).
Axes of the slice: x: 2, y: 2, z: 4, core: 2. Of those that a mesh axis runs over, the one named last changes fastest.
Arguments:
- layer_inputs: bfloat16 [4, 1024, 4096], P('fsdp', 'seq'), may hold values from -8 to 8
- queries: bfloat16 [4, 1024, 4096], P('fsdp', 'seq'), may hold values from -6 to 6
- key_states: bfloat16 [4, 1024, 512], P('fsdp', 'seq'), may hold values from -4 to 4
- value_states: bfloat16 [4, 1024, 512], P('fsdp', 'seq'), may hold values from -1.75 to 1.75
- output_gradient: bfloat16 [4, 1024, 4096], P('fsdp', 'seq'), may hold values from -1.75 to 1.75
- doc_blocks: int32 [4, 4], P('fsdp'), may hold values from 1 to 3, 8 in all within a row
Outputs:
- query_grad: bfloat16 [4, 1024, 4096], P('fsdp', 'seq')
- key_grad: bfloat16 [4, 1024, 512], P('fsdp', 'seq')
- value_grad: bfloat16 [4, 1024, 512], P('fsdp', 'seq')
- value_weight_grad: bfloat16 [4096, 512], P('fsdp')
Inputs may be any that keep to these rules, and one draw needn't show every extreme that they name: `doc_blocks`: the lengths of each packed row sum to 8, and each row has a document of exactly 3 blocks.
All inputs are finite; a program needn't handle non-finite values.
Results may differ from a plain program's by a relative error of at most 0.017.
Values may be sent and summed in bfloat16 or wider, within the bound.
A program may use at most 64 MiB of HBM per device.

v0:
```python
import math
import jax
import jax.numpy as jnp
from jax import lax
from jax.sharding import PartitionSpec as P

KEY_VALUE_HEADS = 4
HEAD_SIZE = 128
BLOCK = 128
QUERY_PER_KEY = 8
BACK = 2
KEYS = 384


def passed_along(x, axis, by):
    peers = lax.axis_size(axis)
    pairs = [(i, i + by) for i in range(peers) if 0 <= i + by < peers]
    return lax.ppermute(x, axis, pairs)


def document_ids(positions, doc_ends):
    block_ids = jnp.floor_divide(positions, BLOCK)
    return jnp.sum((block_ids[:, None] >= doc_ends[None, :]).astype(jnp.int32), axis=1)


def group_grads(q_group, g_group, k_group, v_group, visible, softmax_factor_scale):
    scores = (
        jnp.einsum("rhd,kd->hrk", q_group, k_group, preferred_element_type=jnp.float32)
        * softmax_factor_scale
    )
    scores = jnp.where(visible[None], scores, -jnp.inf)
    row_max = jnp.max(scores, axis=-1, keepdims=True)
    exps = jnp.exp(scores - row_max)
    probs = exps / jnp.sum(exps, axis=-1, keepdims=True)
    d_probs = jnp.einsum("rhd,kd->hrk", g_group, v_group, preferred_element_type=jnp.float32)
    deltas = jnp.sum(probs * d_probs, axis=-1, keepdims=True)
    score_gradient = (probs * (d_probs - deltas)).astype(jnp.bfloat16)
    probability_reduced = probs.astype(jnp.bfloat16)
    value_portion = jnp.einsum(
        "hrk,rhd->kd", probability_reduced, g_group, preferred_element_type=jnp.float32
    )
    key_portion = (
        jnp.einsum("hrk,rhd->kd", score_gradient, q_group, preferred_element_type=jnp.float32)
        * softmax_factor_scale
    )
    query_portion = (
        jnp.einsum("hrk,kd->rhd", score_gradient, k_group, preferred_element_type=jnp.float32)
        * softmax_factor_scale
    )
    return (query_portion, key_portion, value_portion)


def shards(layer_inputs, queries, key_states, value_states, output_gradient, doc_blocks):
    token_rows = queries.shape[1]
    my_index = lax.axis_index("seq")
    own_keys = key_states[0]
    own_values = value_states[0]
    pad_rows = BACK * token_rows
    key_blocks = []
    value_blocks = []
    for distance in range(BACK, 0, -1):
        got_keys, got_values = passed_along((own_keys, own_values), "seq", distance)
        key_blocks.append(got_keys)
        value_blocks.append(got_values)
    key_blocks.append(own_keys)
    value_blocks.append(own_values)
    window_keys = jnp.concatenate(key_blocks, axis=0)
    window_values = jnp.concatenate(value_blocks, axis=0)
    doc_ends = jnp.cumsum(doc_blocks[0])
    first_query = my_index * token_rows
    q_pos = first_query + jnp.arange(token_rows, dtype=jnp.int32)
    k_pos = first_query - pad_rows + jnp.arange(KEYS, dtype=jnp.int32)
    same_doc = document_ids(k_pos, doc_ends)[None, :] == document_ids(q_pos, doc_ends)[:, None]
    visible = same_doc & (k_pos[None, :] >= 0) & (k_pos[None, :] <= q_pos[:, None])
    softmax_factor_scale = 1.0 / math.sqrt(HEAD_SIZE)
    query_head_states = queries[0].reshape(token_rows, KEY_VALUE_HEADS, QUERY_PER_KEY, HEAD_SIZE)
    gradient_heads = output_gradient[0].reshape(
        token_rows, KEY_VALUE_HEADS, QUERY_PER_KEY, HEAD_SIZE
    )
    query_portions = []
    key_parts = []
    value_parts = []
    for key_value_group in range(KEY_VALUE_HEADS):
        k_group = window_keys[:, key_value_group * HEAD_SIZE : (key_value_group + 1) * HEAD_SIZE]
        v_group = window_values[:, key_value_group * HEAD_SIZE : (key_value_group + 1) * HEAD_SIZE]
        query_portion, key_portion, value_portion = group_grads(
            query_head_states[:, key_value_group],
            gradient_heads[:, key_value_group],
            k_group,
            v_group,
            visible,
            softmax_factor_scale,
        )
        query_portions.append(query_portion)
        key_parts.append(key_portion)
        value_parts.append(value_portion)
    query_grad = (
        jnp.stack(query_portions, axis=1)
        .reshape(token_rows, KEY_VALUE_HEADS * QUERY_PER_KEY * HEAD_SIZE)
        .astype(jnp.bfloat16)
    )
    key_window = jnp.concatenate(key_parts, axis=1)
    value_window = jnp.concatenate(value_parts, axis=1)
    key_total = key_window[pad_rows:]
    value_total = value_window[pad_rows:]
    for distance in range(1, BACK + 1):
        lower = (BACK - distance) * token_rows
        got_keys, got_values = (
            passed_along(
                key_window[lower : lower + token_rows].astype(jnp.bfloat16), "seq", -distance
            ).astype(jnp.float32),
            passed_along(
                value_window[lower : lower + token_rows].astype(jnp.bfloat16), "seq", -distance
            ).astype(jnp.float32),
        )
        key_total = key_total + got_keys
        value_total = value_total + got_values
    key_grad = key_total.astype(jnp.bfloat16)
    value_grad = value_total.astype(jnp.bfloat16)
    local_inputs = layer_inputs[0]
    weight_share = lax.psum_scatter(
        lax.dot_general(
            local_inputs, value_grad, (((0,), (0,)), ((), ())), preferred_element_type=jnp.float32
        ).astype(jnp.bfloat16),
        "fsdp",
        scatter_dimension=0,
        tiled=True,
    )
    weight_total = lax.psum(weight_share, "seq").astype(jnp.float32)
    token_count = lax.axis_size("fsdp") * lax.axis_size("seq") * token_rows
    value_weight_grad = (weight_total / math.sqrt(token_count)).astype(jnp.bfloat16)
    return (query_grad[None], key_grad[None], value_grad[None], value_weight_grad)


def solution(mesh):
    placed = (
        P("fsdp", "seq", None),
        P("fsdp", "seq", None),
        P("fsdp", "seq", None),
        P("fsdp", "seq", None),
        P("fsdp", "seq", None),
        P("fsdp", None),
    )
    return jax.shard_map(
        shards,
        mesh=mesh,
        in_specs=placed,
        out_specs=(
            P("fsdp", "seq", None),
            P("fsdp", "seq", None),
            P("fsdp", "seq", None),
            P("fsdp", None),
        ),
        check_vma=False,
    )
```

profile of v0, /device:TPU:0, one launch (start us, length us, event | category | flops | bytes accessed | tf_op | source)
XLA Modules:
  0.0 170.2 jit_solution(6440243550890889599)
XLA Ops:
  7.2 2.5 %collective-permute-start.1 = (bf16[128,512]{1,0:T(8,128)(2,1)}, bf16[128,512]{1,0:T(8,128)(2,1)S(1)}, u32[]{:S(2)}, u32[]{:S(2)}) collective-permute-start(bf16[128,512]{1,0:T(8,128)(2,1)} %bitcast.294), channel_id=1, source_target_pairs={{0,4},{4,8},{8,12},{12,16},{16,20},{20,24},{24,28},{1,5},{5,9},{9,... | collective-permute-start | bytes 393224 | tf_op jit(solution)/shard_map/ppermute | solution.py:18
  9.8 4.5 %collective-permute-start = (bf16[128,512]{1,0:T(8,128)(2,1)}, bf16[128,512]{1,0:T(8,128)(2,1)S(1)}, u32[]{:S(2)}, u32[]{:S(2)}) collective-permute-start(bf16[128,512]{1,0:T(8,128)(2,1)} %bitcast.295), channel_id=1, source_target_pairs={{0,8},{4,12},{8,16},{12,20},{16,24},{20,28},{1,9},{5,13},{9,17},{1... | collective-permute-start | bytes 393224 | tf_op jit(solution)/shard_map/ppermute | solution.py:18
  14.3 0.8 reduce-window.8
  15.2 0.6 convert_reduce_fusion.1
  15.9 1.6 copy.76
  17.5 1.3 copy.78
  18.8 0.9 compare_and_fusion
  19.8 1.8 %fusion.72 = (f32[8,128]{1,0:T(8,128)S(1)}, f32[8,128,384]{1,2,0:T(8,128)}) fusion(pred[128,384]{0,1:T(8,128)(4,1)S(1)} %compare_and_fusion, bf16[128,4,8,128]{0,3,2,1:T(8,128)(2,1)S(1)} %bitcast.276, bf16[384,512]{1,0:T(8,128)(2,1)S(1)} %pad_maximum_fusion.3), kind=kOutput, calls=%fused_computation.139 | convolution fusion | flops 102236544 | bytes 1986560 | tf_op jit(solution)/shard_map/sub | solution.py:33
  21.6 1.8 %fusion.73 = (f32[8,128]{1,0:T(8,128)S(1)}, f32[8,128,384]{1,2,0:T(8,128)}) fusion(pred[128,384]{0,1:T(8,128)(4,1)S(1)} %compare_and_fusion, bf16[128,4,8,128]{0,3,2,1:T(8,128)(2,1)S(1)} %bitcast.277, bf16[384,512]{1,0:T(8,128)(2,1)S(1)} %pad_maximum_fusion.3), kind=kOutput, calls=%fused_computation.140 | convolution fusion | flops 102236544 | bytes 1986560 | tf_op jit(solution)/shard_map/sub | solution.py:33
  23.4 1.8 %fusion.74 = (f32[8,128]{1,0:T(8,128)S(1)}, f32[8,128,384]{1,2,0:T(8,128)}) fusion(pred[128,384]{0,1:T(8,128)(4,1)S(1)} %compare_and_fusion, bf16[128,4,8,128]{0,3,2,1:T(8,128)(2,1)S(1)} %bitcast.278, bf16[384,512]{1,0:T(8,128)(2,1)S(1)} %pad_maximum_fusion.3), kind=kOutput, calls=%fused_computation.141 | convolution fusion | flops 102236544 | bytes 1986560 | tf_op jit(solution)/shard_map/sub | solution.py:33
  25.1 1.8 %fusion.71 = (f32[8,128]{1,0:T(8,128)S(1)}, f32[8,128,384]{1,2,0:T(8,128)}) fusion(pred[128,384]{0,1:T(8,128)(4,1)S(1)} %compare_and_fusion, bf16[128,4,8,128]{0,3,2,1:T(8,128)(2,1)S(1)} %bitcast.279, bf16[384,512]{1,0:T(8,128)(2,1)S(1)} %pad_maximum_fusion.3), kind=kOutput, calls=%fused_computation.138 | convolution fusion | flops 102236544 | bytes 1986560 | tf_op jit(solution)/shard_map/sub | solution.py:33
  26.9 1.9 %convolution_bitcast_fusion.1 = f32[384,128]{0,1:T(8,128)S(1)} fusion(bf16[128,4,8,128]{0,3,2,1:T(8,128)(2,1)} %bitcast.286, f32[8,128,384]{1,2,0:T(8,128)} %get-tuple-element.25, f32[8,128]{1,0:T(8,128)S(1)} %get-tuple-element.24), kind=kOutput, calls=%fused_computation.52 | convolution fusion | flops 101449728 | bytes 2035712 | tf_op jit(solution)/shard_map/hrk,rhd->kd/dot_general | solution.py:39
  29.2 0.4 convolution_bitcast_fusion.2
  29.6 1.0 copy-done.9
  30.6 0.4 convolution_bitcast_fusion.3
  31.0 1.0 copy-done.11
  32.0 0.4 convolution_bitcast_fusion
  32.5 1.3 collective-permute-start.6
  33.8 1.3 collective-permute-start.7
  35.1 1.5 collective-permute-done.6
  36.6 6.5 %collective-permute-done.7 = bf16[128,512]{0,1:T(8,128)(2,1)S(1)} collective-permute-done((bf16[128,512]{0,1:T(8,128)(2,1)S(1)}, bf16[128,512]{0,1:T(8,128)(2,1)S(1)}, u32[]{:S(2)}, u32[]{:S(2)}) %collective-permute-start.7) | collective-permute-done | bytes 131104 | tf_op jit(solution)/shard_map/ppermute | solution.py:18
  43.2 3.2 %fusion.4 = bf16[4096,512]{0,1:T(8,128)(2,1)} fusion(bf16[128,512]{0,1:T(8,128)(2,1)S(1)} %fusion.43, bf16[1,128,4096]{2,1,0:T(8,128)(2,1)S(1)} %copy-done), kind=kOutput, calls=%fused_computation.5 | convolution fusion | flops 538968064 | bytes 5373952 | tf_op jit(solution)/shard_map/dot_general | solution.py:122
  46.4 0.8 copy-done.21
  47.3 1.5 collective-permute-start.3
  48.8 3.9 %collective-permute-start.2 = (bf16[128,512]{1,0:T(8,128)(2,1)S(1)}, bf16[128,512]{1,0:T(8,128)(2,1)S(1)}, u32[]{:S(2)}, u32[]{:S(2)}) collective-permute-start(bf16[128,512]{1,0:T(8,128)(2,1)S(1)} %bitcast.298), channel_id=1, source_target_pairs={{0,8},{4,12},{8,16},{12,20},{16,24},{20,28},{1,9},{5,13},{9,17},{1... | collective-permute-start | bytes 393224 | tf_op jit(solution)/shard_map/ppermute | solution.py:18
  52.7 3.6 %collective-permute-done.2 = bf16[128,512]{1,0:T(8,128)(2,1)S(1)} collective-permute-done((bf16[128,512]{1,0:T(8,128)(2,1)S(1)}, bf16[128,512]{1,0:T(8,128)(2,1)S(1)}, u32[]{:S(2)}, u32[]{:S(2)}) %collective-permute-start.2) | collective-permute-done | bytes 131104 | tf_op jit(solution)/shard_map/ppermute | solution.py:18
  56.3 1.4 fusion.12
  58.3 0.8 copy-done.14
  59.5 0.4 fusion.15
  60.4 0.8 copy-done.12
  61.3 0.4 fusion.9
  61.9 0.8 copy-done.8
  63.4 0.4 fusion.18
  64.3 1.1 pad_maximum_fusion
  65.4 2.3 %copy.110 = bf16[1,128,4096]{2,1,0:T(8,128)(2,1)} copy(bf16[1,128,4096]{1,2,0:T(8,128)(2,1)} %bitcast.284) | data formatting | bytes 2097152
  67.7 1.5 fusion.34
  69.2 1.4 fusion.35
  70.6 0.4 fusion.36
  71.0 0.4 fusion.33
  71.4 27.5 %reduce-scatter.2.cloned.1.call-done = bf16[1024,512]{0,1:T(8,128)(2,1)} async-done(((bf16[4096,512]{0,1:T(8,128)(2,1)}), bf16[1024,512]{0,1:T(8,128)(2,1)}) %reduce-scatter.2.cloned.1.call-update) | async-done | bytes 1048592 | tf_op jit(solution)/shard_map/reduce_scatter | solution.py:121
  99.0 1.3 collective-permute-start.4
  100.3 1.3 collective-permute-start.5
  101.7 0.8 copy.112
  102.5 6.2 %collective-permute-done.5 = bf16[128,512]{0,1:T(8,128)(2,1)S(1)} collective-permute-done((bf16[128,512]{0,1:T(8,128)(2,1)S(1)}, bf16[128,512]{0,1:T(8,128)(2,1)S(1)}, u32[]{:S(2)}, u32[]{:S(2)}) %collective-permute-start.5) | collective-permute-done | bytes 131104 | tf_op jit(solution)/shard_map/ppermute | solution.py:18
  108.7 0.8 copy.111
  109.4 51.2 %all-reduce.2.cloned.1.call-done = bf16[1024,512]{0,1:T(8,128)(2,1)} async-done(((bf16[1024,512]{0,1:T(8,128)(2,1)}), bf16[1024,512]{0,1:T(8,128)(2,1)}) %all-reduce.2.cloned.1.call-update) | async-done | bytes 1048592 | tf_op jit(solution)/shard_map/psum | solution.py:129
  160.6 1.4 multiply_convert_fusion
  162.0 1.3 copy.113
  (70 shorter events, 3.8 us)
Async XLA Ops:
  7.2 36.0 %copy-start = (bf16[1,128,4096]{2,1,0:T(8,128)(2,1)S(1)}, bf16[1,128,4096]{2,1,0:T(8,128)(2,1)}, u32[]{:S(2)}) copy-start(bf16[1,128,4096]{2,1,0:T(8,128)(2,1)} %param.6) | copy-start | bytes 3145732
  7.2 10.3 %copy-start.17 = (bf16[1,128,4096]{2,1,0:T(8,128)(2,1)S(1)}, bf16[1,128,4096]{2,1,0:T(8,128)(2,1)}, u32[]{:S(2)}) copy-start(bf16[1,128,4096]{2,1,0:T(8,128)(2,1)} %param.10) | copy-start | bytes 3145732
  7.2 91.8 %reduce-scatter.2.cloned.1.call-start = ((), (), s32[]{:S(2)}) async-start(), calls=%async_computation.1 | async-start | bytes 5242880 | tf_op jit(solution)/shard_map/reduce_scatter | solution.py:121
  7.2 12.5 %collective-permute-start.1 = (bf16[128,512]{1,0:T(8,128)(2,1)}, bf16[128,512]{1,0:T(8,128)(2,1)S(1)}, u32[]{:S(2)}, u32[]{:S(2)}) collective-permute-start(bf16[128,512]{1,0:T(8,128)(2,1)} %bitcast.294), channel_id=1, source_target_pairs={{0,4},{4,8},{8,12},{12,16},{16,20},{20,24},{24,28},{1,5},{5,9},{9,... | collective-permute-start | bytes 393224 | tf_op jit(solution)/shard_map/ppermute | solution.py:18
  9.8 9.9 %collective-permute-start = (bf16[128,512]{1,0:T(8,128)(2,1)}, bf16[128,512]{1,0:T(8,128)(2,1)S(1)}, u32[]{:S(2)}, u32[]{:S(2)}) collective-permute-start(bf16[128,512]{1,0:T(8,128)(2,1)} %bitcast.295), channel_id=1, source_target_pairs={{0,8},{4,12},{8,16},{12,20},{16,24},{20,28},{1,9},{5,13},{9,17},{1... | collective-permute-start | bytes 393224 | tf_op jit(solution)/shard_map/ppermute | solution.py:18
  17.5 7.7 %copy-start.3 = (bf16[1,128,4096]{1,2,0:T(8,128)(2,1)}, bf16[1,128,4096]{1,2,0:T(8,128)(2,1)S(1)}, u32[]{:S(2)}) copy-start(bf16[1,128,4096]{1,2,0:T(8,128)(2,1)S(1)} %copy.76) | copy-start | bytes 3145732
  17.5 2.2 %copy-start.20 = (bf16[1,128,512]{2,1,0:T(8,128)(2,1)S(1)}, bf16[1,128,512]{2,1,0:T(8,128)(2,1)}, u32[]{:S(2)}) copy-start(bf16[1,128,512]{2,1,0:T(8,128)(2,1)} %param.8) | copy-start | bytes 393220
  19.8 40.3 %copy-start.7 = (bf16[384,512]{1,0:T(8,128)(2,1)}, bf16[384,512]{1,0:T(8,128)(2,1)S(1)}, u32[]{:S(2)}) copy-start(bf16[384,512]{1,0:T(8,128)(2,1)S(1)} %pad_maximum_fusion.3) | copy-start | bytes 1179652
  26.9 2.0 %copy-start.13 = (f32[8,128,384]{1,2,0:T(8,128)S(1)}, f32[8,128,384]{1,2,0:T(8,128)}, u32[]{:S(2)}) copy-start(f32[8,128,384]{1,2,0:T(8,128)} %get-tuple-element.29) | copy-start | bytes 4718596
  26.9 2.2 %copy-start.18 = (bf16[1,128,4096]{1,2,0:T(8,128)(2,1)S(1)}, bf16[1,128,4096]{1,2,0:T(8,128)(2,1)}, u32[]{:S(2)}) copy-start(bf16[1,128,4096]{1,2,0:T(8,128)(2,1)} %copy.78) | copy-start | bytes 3145732
  29.2 1.4 copy-start.9
  30.6 1.4 copy-start.11
  32.5 4.1 %collective-permute-start.6 = (bf16[128,512]{0,1:T(8,128)(2,1)S(1)}, bf16[128,512]{0,1:T(8,128)(2,1)S(1)}, u32[]{:S(2)}, u32[]{:S(2)}) collective-permute-start(bf16[128,512]{0,1:T(8,128)(2,1)S(1)} %get-tuple-element.16), channel_id=1, source_target_pairs={{4,0},{8,4},{12,8},{16,12},{20,16},{24,20},{28,24},{5,1},{9,5},{13... | collective-permute-start | bytes 393224 | tf_op jit(solution)/shard_map/ppermute | solution.py:18
  33.8 9.4 %collective-permute-start.7 = (bf16[128,512]{0,1:T(8,128)(2,1)S(1)}, bf16[128,512]{0,1:T(8,128)(2,1)S(1)}, u32[]{:S(2)}, u32[]{:S(2)}) collective-permute-start(bf16[128,512]{0,1:T(8,128)(2,1)S(1)} %get-tuple-element.17), channel_id=1, source_target_pairs={{8,0},{12,4},{16,8},{20,12},{24,16},{28,20},{9,1},{13,5},{17,9},{2... | collective-permute-start | bytes 393224 | tf_op jit(solution)/shard_map/ppermute | solution.py:18
  46.4 0.9 copy-start.21
  46.4 9.9 %copy-start.15 = (f32[8,128,384]{1,2,0:T(8,128)S(1)}, f32[8,128,384]{1,2,0:T(8,128)}, u32[]{:S(2)}) copy-start(f32[8,128,384]{1,2,0:T(8,128)} %get-tuple-element.25) | copy-start | bytes 4718596
  46.4 114.2 %all-reduce.2.cloned.1.call-start = ((), (), s32[]{:S(2)}) async-start(), calls=%async_computation.2 | async-start | bytes 2097152 | tf_op jit(solution)/shard_map/psum | solution.py:129
  47.3 5.4 %collective-permute-start.3 = (bf16[128,512]{1,0:T(8,128)(2,1)S(1)}, bf16[128,512]{1,0:T(8,128)(2,1)S(1)}, u32[]{:S(2)}, u32[]{:S(2)}) collective-permute-start(bf16[128,512]{1,0:T(8,128)(2,1)S(1)} %bitcast.297), channel_id=1, source_target_pairs={{0,4},{4,8},{8,12},{12,16},{16,20},{20,24},{24,28},{1,5},{5,9},{9,... | collective-permute-start | bytes 393224 | tf_op jit(solution)/shard_map/ppermute | solution.py:18
  48.8 7.5 %collective-permute-start.2 = (bf16[128,512]{1,0:T(8,128)(2,1)S(1)}, bf16[128,512]{1,0:T(8,128)(2,1)S(1)}, u32[]{:S(2)}, u32[]{:S(2)}) collective-permute-start(bf16[128,512]{1,0:T(8,128)(2,1)S(1)} %bitcast.298), channel_id=1, source_target_pairs={{0,8},{4,12},{8,16},{12,20},{16,24},{20,28},{1,9},{5,13},{9,17},{1... | collective-permute-start | bytes 393224 | tf_op jit(solution)/shard_map/ppermute | solution.py:18
  56.3 1.5 copy-start.16
  57.8 1.4 copy-start.14
  57.8 1.7 copy-start.19
  59.9 1.4 copy-start.12
  61.6 1.1 copy-start.8
  61.6 1.7 %copy-start.10 = (f32[8,128,384]{1,2,0:T(8,128)S(1)}, f32[8,128,384]{1,2,0:T(8,128)}, u32[]{:S(2)}) copy-start(f32[8,128,384]{1,2,0:T(8,128)} %get-tuple-element.33) | copy-start | bytes 4718596
  64.0 1.4 copy-start.1
  67.7 2.9 %copy-start.2 = (bf16[8,128,384]{1,2,0:T(8,128)(2,1)S(1)}, bf16[8,128,384]{1,2,0:T(8,128)(2,1)}, u32[]{:S(2)}) copy-start(bf16[8,128,384]{1,2,0:T(8,128)(2,1)} %copy-done.1) | copy-start | bytes 2359300
  67.7 2.9 %copy-start.4 = (bf16[1,128,4096]{1,2,0:T(8,128)(2,1)S(1)}, bf16[1,128,4096]{1,2,0:T(8,128)(2,1)}, u32[]{:S(2)}) copy-start(bf16[1,128,4096]{1,2,0:T(8,128)(2,1)} %copy-done.3) | copy-start | bytes 3145732
  69.2 2.2 %copy-start.5 = (f32[384,128]{0,1:T(8,128)}, f32[384,128]{0,1:T(8,128)S(1)}, u32[]{:S(2)}) copy-start(f32[384,128]{0,1:T(8,128)S(1)} %fusion.34) | copy-start | bytes 589828
  71.4 30.2 %copy-start.6 = (f32[384,128]{0,1:T(8,128)S(1)}, f32[384,128]{0,1:T(8,128)}, u32[]{:S(2)}) copy-start(f32[384,128]{0,1:T(8,128)} %copy-done.5) | copy-start | bytes 589828
  99.0 3.4 %collective-permute-start.4 = (bf16[128,512]{0,1:T(8,128)(2,1)S(1)}, bf16[128,512]{0,1:T(8,128)(2,1)S(1)}, u32[]{:S(2)}, u32[]{:S(2)}) collective-permute-start(bf16[128,512]{0,1:T(8,128)(2,1)S(1)} %get-tuple-element.18), channel_id=1, source_target_pairs={{4,0},{8,4},{12,8},{16,12},{20,16},{24,20},{28,24},{5,1},{9,5},{13... | collective-permute-start | bytes 393224 | tf_op jit(solution)/shard_map/ppermute | solution.py:18
  100.3 8.3 %collective-permute-start.5 = (bf16[128,512]{0,1:T(8,128)(2,1)S(1)}, bf16[128,512]{0,1:T(8,128)(2,1)S(1)}, u32[]{:S(2)}, u32[]{:S(2)}) collective-permute-start(bf16[128,512]{0,1:T(8,128)(2,1)S(1)} %get-tuple-element.19), channel_id=1, source_target_pairs={{8,0},{12,4},{16,8},{20,12},{24,16},{28,20},{9,1},{13,5},{17,9},{2... | collective-permute-start | bytes 393224 | tf_op jit(solution)/shard_map/ppermute | solution.py:18
Sparse Core Ops, SparseCore 0:
  46.5 52.3 reduce-scatter.1
  101.3 59.2 all-reduce.1
where the time goes:
time: 171 us; the launch traced here: 170 us
  waiting for transfers between devices  96.5 us (56%)
  matrix products  20.8 us (12%)
  starting transfers between devices  17.7 us (10%)
  between operations  14.6 us (9%)
  local copies, waits for them, and re-layouts  14.5 us (8%)
  other arithmetic  6.15 us (4%)
    psum x1, waiting for transfers between devices, shards(): weight_total = lax.psum(weight_share, 'seq').astype(jnp.float32)  51.2 us
    reduce_scatter x1, waiting for transfers between devices, shards(): lax.psum_scatter(lax.dot_general(local_inputs, value_grad, (((0,), (0,)),...  27.5 us
    ppermute x8, waiting for transfers between devices, passed_along(): return lax.ppermute(x, axis, pairs)  17.8 us
    ppermute x8, starting transfers between devices, passed_along(): return lax.ppermute(x, axis, pairs)  17.6 us
    unnamed x50, local copies, waits for them, and re-layouts  14.5 us
    sub x4, matrix products, group_grads(): exps = jnp.exp(scores - row_max)  7.15 us
    dot_general x4, matrix products, group_grads(): jnp.einsum('hrk,rhd->kd', score_gradient, q_group, preferred_element_type...  3.6 us
  transfers between devices with their start and end apart: 10, of which 6 were waited for; matrix products, arithmetic and copies ran while one was open for 11% of the time, Pallas kernels for 0%

commit v1 on v0

--- a/solution.py
+++ b/solution.py
@@ -126,7 +126,7 @@
         scatter_dimension=0,
         tiled=True,
     )
-    weight_total = lax.psum(weight_share, "seq").astype(jnp.float32)
+    weight_total = jnp.sum(lax.all_gather(weight_share, "seq"), axis=0).astype(jnp.float32)
     token_count = lax.axis_size("fsdp") * lax.axis_size("seq") * token_rows
     value_weight_grad = (weight_total / math.sqrt(token_count)).astype(jnp.bfloat16)
     return (query_grad[None], key_grad[None], value_grad[None], value_weight_grad)

time: 171 us -> 223 us (1.30)
  waiting for transfers between devices: 96.5 us -> 123 us
  local copies, waits for them, and re-layouts: 14.5 us -> 30.6 us
  other arithmetic: 6.15 us -> 15.8 us
    psum x1 -> x0, waiting for transfers between devices: 51.2 us -> none  [shards(): weight_total = lax.psum(weight_share, 'seq').astype(jnp.float32)]
    all_gather x0 -> x1, waiting for transfers between devices: none -> 40.1 us  [shards(): lax.all_gather(weight_share, 'seq')]
    reduce_scatter x1, waiting for transfers between devices: 27.5 us -> 52.5 us  [shards(): lax.psum_scatter(lax.dot_general(local_inputs, value_grad, (((0,), (0,)),...]
    unnamed x50 -> x47, local copies, waits for them, and re-layouts: 14.5 us -> 30.5 us
    ppermute x8, waiting for transfers between devices: 17.8 us -> 30.2 us  [passed_along(): return lax.ppermute(x, axis, pairs)]
    reduce_sum x0 -> x1, other arithmetic: none -> 10.9 us  [shards(): jnp.sum(lax.all_gather(weight_share, 'seq'), axis=0).astype(jnp.float32)]
  transfers between devices with their start and end apart: 10 -> 10, of which waited for: 6 -> 6; matrix products, arithmetic and copies ran while one was open for 11% -> 8% of each run, Pallas kernels for 0% -> 0%
where the time goes in v1:
time: 223 us; the launch traced here: 222 us
  waiting for transfers between devices  123 us (55%)
  local copies, waits for them, and re-layouts  30.6 us (14%)
  matrix products  20.7 us (9%)
  starting transfers between devices  17.8 us (8%)
  other arithmetic  15.8 us (7%)
  between operations  14.6 us (7%)
    reduce_scatter x1, waiting for transfers between devices, shards(): lax.psum_scatter(lax.dot_general(local_inputs, value_grad, (((0,), (0,)),...  52.5 us
    all_gather x1, waiting for transfers between devices, shards(): lax.all_gather(weight_share, 'seq')  40.1 us
    unnamed x47, local copies, waits for them, and re-layouts  30.5 us
    ppermute x8, waiting for transfers between devices, passed_along(): return lax.ppermute(x, axis, pairs)  30.2 us
    ppermute x8, starting transfers between devices, passed_along(): return lax.ppermute(x, axis, pairs)  17.7 us
    reduce_sum x1, other arithmetic, shards(): jnp.sum(lax.all_gather(weight_share, 'seq'), axis=0).astype(jnp.float32)  10.9 us
    sub x4, matrix products, group_grads(): exps = jnp.exp(scores - row_max)  7.08 us
  transfers between devices with their start and end apart: 10, of which 6 were waited for; matrix products, arithmetic and copies ran while one was open for 8% of the time, Pallas kernels for 0%

profile of v1, /device:TPU:0, one launch (start us, length us, event | category | flops | bytes accessed | tf_op | source)
XLA Modules:
  0.0 222.2 jit_solution(8977055975731507136)
XLA Ops:
  7.2 2.5 %collective-permute-start.1 = (bf16[128,512]{1,0:T(8,128)(2,1)}, bf16[128,512]{1,0:T(8,128)(2,1)S(1)}, u32[]{:S(2)}, u32[]{:S(2)}) collective-permute-start(bf16[128,512]{1,0:T(8,128)(2,1)} %bitcast.300), channel_id=1, source_target_pairs={{0,4},{4,8},{8,12},{12,16},{16,20},{20,24},{24,28},{1,5},{5,9},{9,... | collective-permute-start | bytes 393224 | tf_op jit(solution)/shard_map/ppermute | solution.py:18
  9.8 4.5 %collective-permute-start = (bf16[128,512]{1,0:T(8,128)(2,1)}, bf16[128,512]{1,0:T(8,128)(2,1)S(1)}, u32[]{:S(2)}, u32[]{:S(2)}) collective-permute-start(bf16[128,512]{1,0:T(8,128)(2,1)} %bitcast.301), channel_id=1, source_target_pairs={{0,8},{4,12},{8,16},{12,20},{16,24},{20,28},{1,9},{5,13},{9,17},{1... | collective-permute-start | bytes 393224 | tf_op jit(solution)/shard_map/ppermute | solution.py:18
  14.3 0.8 reduce-window.8
  15.2 0.6 convert_reduce_fusion.1
  15.9 1.6 copy.112
  17.5 1.3 copy.114
  18.8 0.9 compare_and_fusion
  19.8 1.7 fusion.72
  21.5 1.8 fusion.73
  23.3 1.8 fusion.74
  25.1 1.7 fusion.71
  26.9 1.9 convolution_bitcast_fusion.1
  29.1 0.4 convolution_bitcast_fusion.2
  29.5 1.0 copy-done.7
  30.5 0.4 convolution_bitcast_fusion.3
  30.9 1.0 copy-done.9
  31.9 0.4 convolution_bitcast_fusion
  32.4 1.3 collective-permute-start.6
  33.7 1.3 collective-permute-start.7
  35.0 1.5 collective-permute-done.6
  36.5 6.5 %collective-permute-done.7 = bf16[128,512]{0,1:T(8,128)(2,1)S(1)} collective-permute-done((bf16[128,512]{0,1:T(8,128)(2,1)S(1)}, bf16[128,512]{0,1:T(8,128)(2,1)S(1)}, u32[]{:S(2)}, u32[]{:S(2)}) %collective-permute-start.7) | collective-permute-done | bytes 131104 | tf_op jit(solution)/shard_map/ppermute | solution.py:18
  43.1 3.2 %fusion.4 = bf16[4096,512]{0,1:T(8,128)(2,1)} fusion(bf16[128,512]{0,1:T(8,128)(2,1)S(1)} %fusion.43, bf16[1,128,4096]{2,1,0:T(8,128)(2,1)S(1)} %copy-done), kind=kOutput, calls=%fused_computation.6 | convolution fusion | flops 538968064 | bytes 5373952 | tf_op jit(solution)/shard_map/dot_general | solution.py:122
  46.4 52.5 %reduce-scatter.2.cloned.1.call-done = bf16[1024,512]{0,1:T(8,128)(2,1)} async-done(((bf16[4096,512]{0,1:T(8,128)(2,1)}), bf16[1024,512]{0,1:T(8,128)(2,1)}) %reduce-scatter.2.cloned.1.call-update) | async-done | bytes 1048592 | tf_op jit(solution)/shard_map/reduce_scatter | solution.py:121
  98.9 1.6 collective-permute-start.3
  100.5 3.7 %collective-permute-start.2 = (bf16[128,512]{1,0:T(8,128)(2,1)S(1)}, bf16[128,512]{1,0:T(8,128)(2,1)S(1)}, u32[]{:S(2)}, u32[]{:S(2)}) collective-permute-start(bf16[128,512]{1,0:T(8,128)(2,1)S(1)} %bitcast.304), channel_id=1, source_target_pairs={{0,8},{4,12},{8,16},{12,20},{16,24},{20,28},{1,9},{5,13},{9,17},{1... | collective-permute-start | bytes 393224 | tf_op jit(solution)/shard_map/ppermute | solution.py:18
  104.2 3.2 %collective-permute-done.2 = bf16[128,512]{1,0:T(8,128)(2,1)S(1)} collective-permute-done((bf16[128,512]{1,0:T(8,128)(2,1)S(1)}, bf16[128,512]{1,0:T(8,128)(2,1)S(1)}, u32[]{:S(2)}, u32[]{:S(2)}) %collective-permute-start.2) | collective-permute-done | bytes 131104 | tf_op jit(solution)/shard_map/ppermute | solution.py:18
  107.5 1.5 fusion.12
  109.8 1.3 copy-done.12
  111.1 0.5 copy-done.17
  112.5 0.8 copy-done.10
  113.3 0.4 fusion.9
  113.9 0.8 copy-done.6
  115.2 0.4 fusion.18
  116.1 1.1 pad_maximum_fusion
  117.2 2.3 %copy.146 = bf16[1,128,4096]{2,1,0:T(8,128)(2,1)} copy(bf16[1,128,4096]{1,2,0:T(8,128)(2,1)} %bitcast.290) | data formatting | bytes 2097152
  119.5 1.5 fusion.34
  121.0 1.3 fusion.35
  122.3 0.4 fusion.36
  122.7 0.4 fusion.33
  123.2 1.3 collective-permute-start.4
  124.5 1.5 collective-permute-start.5
  126.0 0.8 copy.148
  126.8 19.0 %collective-permute-done.5 = bf16[128,512]{0,1:T(8,128)(2,1)S(1)} collective-permute-done((bf16[128,512]{0,1:T(8,128)(2,1)S(1)}, bf16[128,512]{0,1:T(8,128)(2,1)S(1)}, u32[]{:S(2)}, u32[]{:S(2)}) %collective-permute-start.5) | collective-permute-done | bytes 131104 | tf_op jit(solution)/shard_map/ppermute | solution.py:18
  145.8 0.8 copy.147
  146.6 40.1 %all-gather.3.cloned.1.call-done = bf16[8192,512]{0,1:T(8,128)(2,1)} async-done(((bf16[1024,512]{0,1:T(8,128)(2,1)}), bf16[8192,512]{0,1:T(8,128)(2,1)}) %all-gather.3.cloned.1.call-update) | async-done | bytes 8388624 | tf_op jit(solution)/shard_map/all_gather | solution.py:129
  186.7 16.3 %copy.186 = bf16[64,8,8,1024]{3,2,1,0:T(8,128)(2,1)} copy(bf16[64,8,8,1024]{3,1,2,0:T(8,128)(2,1)} %bitcast.281) | data formatting | bytes 16777216
  203.0 10.9 %bitcast_reduce_fusion = bf16[1024,512]{0,1:T(8,128)(2,1)S(1)} fusion(bf16[64,8,8,1024]{3,2,1,0:T(8,128)(2,1)} %copy.186), kind=kLoop, calls=%fused_computation.4 | loop fusion | flops 3670016 | bytes 9437184 | tf_op jit(solution)/shard_map/reduce_sum | solution.py:129
  214.1 1.3 copy.149
  (68 shorter events, 4.1 us)
Async XLA Ops:
  7.2 36.0 %copy-start = (bf16[1,128,4096]{2,1,0:T(8,128)(2,1)S(1)}, bf16[1,128,4096]{2,1,0:T(8,128)(2,1)}, u32[]{:S(2)}) copy-start(bf16[1,128,4096]{2,1,0:T(8,128)(2,1)} %param.6) | copy-start | bytes 3145732
  7.2 10.3 %copy-start.15 = (bf16[1,128,4096]{2,1,0:T(8,128)(2,1)S(1)}, bf16[1,128,4096]{2,1,0:T(8,128)(2,1)}, u32[]{:S(2)}) copy-start(bf16[1,128,4096]{2,1,0:T(8,128)(2,1)} %param.10) | copy-start | bytes 3145732
  7.2 91.7 %reduce-scatter.2.cloned.1.call-start = ((), (), s32[]{:S(2)}) async-start(), calls=%async_computation.1 | async-start | bytes 5242880 | tf_op jit(solution)/shard_map/reduce_scatter | solution.py:121
  7.2 12.5 %collective-permute-start.1 = (bf16[128,512]{1,0:T(8,128)(2,1)}, bf16[128,512]{1,0:T(8,128)(2,1)S(1)}, u32[]{:S(2)}, u32[]{:S(2)}) collective-permute-start(bf16[128,512]{1,0:T(8,128)(2,1)} %bitcast.300), channel_id=1, source_target_pairs={{0,4},{4,8},{8,12},{12,16},{16,20},{20,24},{24,28},{1,5},{5,9},{9,... | collective-permute-start | bytes 393224 | tf_op jit(solution)/shard_map/ppermute | solution.py:18
  9.8 9.9 %collective-permute-start = (bf16[128,512]{1,0:T(8,128)(2,1)}, bf16[128,512]{1,0:T(8,128)(2,1)S(1)}, u32[]{:S(2)}, u32[]{:S(2)}) collective-permute-start(bf16[128,512]{1,0:T(8,128)(2,1)} %bitcast.301), channel_id=1, source_target_pairs={{0,8},{4,12},{8,16},{12,20},{16,24},{20,28},{1,9},{5,13},{9,17},{1... | collective-permute-start | bytes 393224 | tf_op jit(solution)/shard_map/ppermute | solution.py:18
  17.5 7.6 %copy-start.3 = (bf16[1,128,4096]{1,2,0:T(8,128)(2,1)}, bf16[1,128,4096]{1,2,0:T(8,128)(2,1)S(1)}, u32[]{:S(2)}) copy-start(bf16[1,128,4096]{1,2,0:T(8,128)(2,1)S(1)} %copy.112) | copy-start | bytes 3145732
  17.5 2.2 copy-start.18
  19.8 92.4 %copy-start.5 = (bf16[384,512]{1,0:T(8,128)(2,1)}, bf16[384,512]{1,0:T(8,128)(2,1)S(1)}, u32[]{:S(2)}) copy-start(bf16[384,512]{1,0:T(8,128)(2,1)S(1)} %pad_maximum_fusion.3) | copy-start | bytes 1179652
  26.9 2.0 copy-start.11
  26.9 2.2 %copy-start.16 = (bf16[1,128,4096]{1,2,0:T(8,128)(2,1)S(1)}, bf16[1,128,4096]{1,2,0:T(8,128)(2,1)}, u32[]{:S(2)}) copy-start(bf16[1,128,4096]{1,2,0:T(8,128)(2,1)} %copy.114) | copy-start | bytes 3145732
  29.1 1.4 copy-start.7
  30.5 1.4 copy-start.9
  32.4 4.1 %collective-permute-start.6 = (bf16[128,512]{0,1:T(8,128)(2,1)S(1)}, bf16[128,512]{0,1:T(8,128)(2,1)S(1)}, u32[]{:S(2)}, u32[]{:S(2)}) collective-permute-start(bf16[128,512]{0,1:T(8,128)(2,1)S(1)} %get-tuple-element.20), channel_id=1, source_target_pairs={{4,0},{8,4},{12,8},{16,12},{20,16},{24,20},{28,24},{5,1},{9,5},{13... | collective-permute-start | bytes 393224 | tf_op jit(solution)/shard_map/ppermute | solution.py:18
  33.7 9.4 %collective-permute-start.7 = (bf16[128,512]{0,1:T(8,128)(2,1)S(1)}, bf16[128,512]{0,1:T(8,128)(2,1)S(1)}, u32[]{:S(2)}, u32[]{:S(2)}) collective-permute-start(bf16[128,512]{0,1:T(8,128)(2,1)S(1)} %get-tuple-element.21), channel_id=1, source_target_pairs={{8,0},{12,4},{16,8},{20,12},{24,16},{28,20},{9,1},{13,5},{17,9},{2... | collective-permute-start | bytes 393224 | tf_op jit(solution)/shard_map/ppermute | solution.py:18
  46.3 52.6 %copy-start.19 = (bf16[1,128,512]{2,1,0:T(8,128)(2,1)S(1)}, bf16[1,128,512]{2,1,0:T(8,128)(2,1)}, u32[]{:S(2)}) copy-start(bf16[1,128,512]{2,1,0:T(8,128)(2,1)} %param.9) | copy-start | bytes 393220
  46.3 61.2 %copy-start.13 = (f32[8,128,384]{1,2,0:T(8,128)S(1)}, f32[8,128,384]{1,2,0:T(8,128)}, u32[]{:S(2)}) copy-start(f32[8,128,384]{1,2,0:T(8,128)} %get-tuple-element.29) | copy-start | bytes 4718596
  46.3 140.3 %all-gather.3.cloned.1.call-start = ((), (), s32[]{:S(2)}) async-start(), calls=%async_computation.2 | async-start | bytes 9437184 | tf_op jit(solution)/shard_map/all_gather | solution.py:129
  98.9 5.3 %collective-permute-start.3 = (bf16[128,512]{1,0:T(8,128)(2,1)S(1)}, bf16[128,512]{1,0:T(8,128)(2,1)S(1)}, u32[]{:S(2)}, u32[]{:S(2)}) collective-permute-start(bf16[128,512]{1,0:T(8,128)(2,1)S(1)} %bitcast.303), channel_id=1, source_target_pairs={{0,4},{4,8},{8,12},{12,16},{16,20},{20,24},{24,28},{1,5},{5,9},{9,... | collective-permute-start | bytes 393224 | tf_op jit(solution)/shard_map/ppermute | solution.py:18
  100.5 7.0 %collective-permute-start.2 = (bf16[128,512]{1,0:T(8,128)(2,1)S(1)}, bf16[128,512]{1,0:T(8,128)(2,1)S(1)}, u32[]{:S(2)}, u32[]{:S(2)}) collective-permute-start(bf16[128,512]{1,0:T(8,128)(2,1)S(1)} %bitcast.304), channel_id=1, source_target_pairs={{0,8},{4,12},{8,16},{12,20},{16,24},{20,28},{1,9},{5,13},{9,17},{1... | collective-permute-start | bytes 393224 | tf_op jit(solution)/shard_map/ppermute | solution.py:18
  107.5 1.7 copy-start.14
  109.2 1.9 copy-start.12
  109.2 2.3 %copy-start.17 = (bf16[1,128,4096]{1,2,0:T(8,128)(2,1)S(1)}, bf16[1,128,4096]{1,2,0:T(8,128)(2,1)}, u32[]{:S(2)}) copy-start(bf16[1,128,4096]{1,2,0:T(8,128)(2,1)} %copy.114) | copy-start | bytes 3145732
  111.9 1.4 copy-start.10
  113.7 1.0 copy-start.6
  113.7 1.5 copy-start.8
  115.8 1.4 copy-start.1
  119.5 2.8 %copy-start.2 = (bf16[8,128,384]{1,2,0:T(8,128)(2,1)S(1)}, bf16[8,128,384]{1,2,0:T(8,128)(2,1)}, u32[]{:S(2)}) copy-start(bf16[8,128,384]{1,2,0:T(8,128)(2,1)} %copy-done.1) | copy-start | bytes 2359300
  119.5 2.8 %copy-start.4 = (bf16[1,128,4096]{1,2,0:T(8,128)(2,1)S(1)}, bf16[1,128,4096]{1,2,0:T(8,128)(2,1)}, u32[]{:S(2)}) copy-start(bf16[1,128,4096]{1,2,0:T(8,128)(2,1)} %copy-done.3) | copy-start | bytes 3145732
  123.2 3.6 %collective-permute-start.4 = (bf16[128,512]{0,1:T(8,128)(2,1)S(1)}, bf16[128,512]{0,1:T(8,128)(2,1)S(1)}, u32[]{:S(2)}, u32[]{:S(2)}) collective-permute-start(bf16[128,512]{0,1:T(8,128)(2,1)S(1)} %get-tuple-element.22), channel_id=1, source_target_pairs={{4,0},{8,4},{12,8},{16,12},{20,16},{24,20},{28,24},{5,1},{9,5},{13... | collective-permute-start | bytes 393224 | tf_op jit(solution)/shard_map/ppermute | solution.py:18
  124.5 21.3 %collective-permute-start.5 = (bf16[128,512]{0,1:T(8,128)(2,1)S(1)}, bf16[128,512]{0,1:T(8,128)(2,1)S(1)}, u32[]{:S(2)}, u32[]{:S(2)}) collective-permute-start(bf16[128,512]{0,1:T(8,128)(2,1)S(1)} %get-tuple-element.23), channel_id=1, source_target_pairs={{8,0},{12,4},{16,8},{20,12},{24,16},{28,20},{9,1},{13,5},{17,9},{2... | collective-permute-start | bytes 393224 | tf_op jit(solution)/shard_map/ppermute | solution.py:18
Sparse Core Ops, SparseCore 0:
  46.4 52.3 reduce-scatter.1
  100.5 86.1 all-gather.2
